TPU v7x, 32 devices: a whole 2x2x4 slice. The times are simulated.
32 devices in a mesh: view: 2 (over y), tile: 4 (over z), slab: 4 (over x, core).
Axes of the slice: x: 2, y: 2, z: 4, core: 2. Of those that a mesh axis runs over, the one named last changes fastest.
Arguments:
- estimate: float32 [64, 64, 128], P('slab', 'tile'), may hold values from 0.5 to 2
- recorded: float32 [2, 64, 64, 128], P('view', 'slab', 'tile'), may hold values from 0.25 to 4
- x_index: int32 [2, 64, 128], P('view', 'slab'), may hold values from 0 to 15
- y_index: int32 [2, 64, 64], P('view', 'slab', 'tile'), may hold values from 0 to 15
- z_index: int32 [2, 64, 128], P('view', 'tile'), may hold values from 0 to 15
- profiles: float32 [2, 3, 16, 31], P('view'), may hold values from 0.01 to 1
Outputs:
- updated: float32 [64, 64, 128], P('slab', 'tile')
All inputs are finite; a program needn't handle non-finite values.
Results may differ from a plain program's by a relative error of at most 0.00005.
Values sent between devices are 32-bit elements; how exact they have to be, the bound alone decides.
A program may use at most 64 MiB of HBM per device.

v0:
```python
import jax
import jax.numpy as jnp
from jax import lax
from jax.sharding import PartitionSpec as P


def with_halo(shard, sides, width):
    for axis, dim in sides:
        devices, length = (lax.axis_size(axis), shard.shape[dim])
        up = [(i, (i + 1) % devices) for i in range(devices - 1)]
        down = [(j, i) for i, j in up]
        last = lax.slice_in_dim(shard, length - width, length, axis=dim)
        initial = lax.slice_in_dim(shard, 0, width, axis=dim)
        before = lax.ppermute(last, axis, up)
        after = lax.ppermute(initial, axis, down)
        shard = jnp.concatenate([before, shard, after], axis=dim)
    return shard


def banded(padded, weights, dim, adjoint):
    count = padded.shape[dim] - 30
    total = None
    for k in range(31):
        start = 30 - k if adjoint else k
        term = weights[..., k] * lax.slice_in_dim(padded, start, start + count, axis=dim)
        total = term if total is None else total + term
    return total


def pad_along(field, dim):
    widths = [(0, 0)] * field.ndim
    widths[dim] = (15, 15)
    return jnp.pad(field, widths)


def lookup(index_map, table):
    levels = jnp.arange(table.shape[1], dtype=jnp.int32)
    onehot = (index_map[..., None] == levels).astype(jnp.float32)
    return jnp.einsum("vabp,vpk->vabk", onehot, table, precision=lax.Precision.HIGHEST)


def z_blur(field, z_taps, adjoint):
    margin = with_halo(field, (("slab", 1),), 15)
    return banded(margin, z_taps[:, None], 1, adjoint)


def shards(estimate, recorded, x_index, y_index, z_index, profiles):
    views_here = recorded.shape[0]
    weights = profiles / jnp.sum(profiles, axis=-1, keepdims=True)
    x_taps = lookup(x_index, weights[:, 0])[:, :, None, :, :]
    y_taps = lookup(y_index, weights[:, 1])[:, :, :, None, :]
    z_taps = lookup(z_index, weights[:, 2])
    widened = with_halo(estimate, (("tile", 1),), 15)
    along_x = banded(widened, x_taps, 1, False)
    along_y = banded(pad_along(along_x, 3), y_taps, 3, False)
    blurred = z_blur(along_y, z_taps, False)
    ratio = recorded / blurred
    back_z = z_blur(ratio, z_taps, True)
    back_y = banded(pad_along(back_z, 3), y_taps, 3, True)
    margin = with_halo(back_y, (("tile", 2),), 15)
    back_x = banded(margin, x_taps, 2, True)
    local_sum = jnp.sum(back_x, axis=0)
    total = lax.psum(local_sum, "view")
    return estimate * total / (views_here * lax.axis_size("view"))


def solution(mesh):
    placed = (
        P("slab", "tile", None),
        P("view", "slab", "tile", None),
        P("view", "slab", None),
        P("view", "slab", "tile"),
        P("view", "tile", None),
        P("view", None, None, None),
    )
    return jax.shard_map(
        shards, mesh=mesh, in_specs=placed, out_specs=P("slab", "tile", None), check_vma=False
    )
```

profile of v0, /device:TPU:0, one launch (start us, length us, event | category | flops | bytes accessed | tf_op | source)
XLA Modules:
  0.0 85.9 jit_solution(4088150595432847791)
XLA Ops:
  6.5 1.0 %fusion.455 = (f32[16,15,128]{2,1,0:T(8,128)S(1)}, f32[16,15,128]{2,1,0:T(8,128)S(1)}) fusion(f32[16,16,128]{2,1,0:T(8,128)} %param.6), kind=kLoop, calls=%fused_computation.777 | loop fusion | bytes 491520 | tf_op jit(solution)/shard_map/slice | solution.py:13
  7.5 1.3 %collective-permute-start.1 = (f32[16,15,128]{2,1,0:T(8,128)S(1)}, f32[16,15,128]{2,1,0:T(8,128)S(1)}, u32[]{:S(2)}, u32[]{:S(2)}) collective-permute-start(f32[16,15,128]{2,1,0:T(8,128)S(1)} %get-tuple-element.104), channel_id=1, source_target_pairs={{4,0},{8,4},{12,8},{5,1},{9,5},{13,9},{6,2},{10,6},{14,10},{7,3},{... | collective-permute-start | bytes 368648 | tf_op jit(solution)/shard_map/ppermute | solution.py:15
  8.8 5.6 %collective-permute-start = (f32[16,15,128]{2,1,0:T(8,128)S(1)}, f32[16,15,128]{2,1,0:T(8,128)S(1)}, u32[]{:S(2)}, u32[]{:S(2)}) collective-permute-start(f32[16,15,128]{2,1,0:T(8,128)S(1)} %get-tuple-element.105), channel_id=1, source_target_pairs={{0,4},{4,8},{8,12},{1,5},{5,9},{9,13},{2,6},{6,10},{10,14},{3,7},{... | collective-permute-start | bytes 368648 | tf_op jit(solution)/shard_map/ppermute | solution.py:14
  14.6 0.6 copy-done.3
  15.8 0.6 copy-done.4
  16.6 1.3 %slice_reduce_fusion.30 = (f32[16,16]{1,0:T(8,128)S(1)}, f32[16,16]{1,0:T(8,128)S(1)}, f32[16,16]{1,0:T(8,128)S(1)}, f32[16,16]{1,0:T(8,128)S(1)}, f32[16,16]{1,...) fusion(f32[1,16,16,1,31]{4,2,1,3,0:T(8,128)S(1)} %convolution_b, ...), kind=kLoop, calls=%fused_computation.756 | loop fusion | bytes 38912 | tf_op jit(solution)/shard_map/slice | solution.py:25
  18.4 0.9 %slice_reduce_fusion.29 = (f32[16,16]{1,0:T(8,128)S(1)}, f32[16,16]{1,0:T(8,128)S(1)}, f32[16,16]{1,0:T(8,128)S(1)}, f32[16,16]{1,0:T(8,128)S(1)}, f32[16,16]{1,...) fusion(f32[1,16,16,1,31]{4,2,1,3,0:T(8,128)S(1)} %convolution_b, ...), kind=kLoop, calls=%fused_computation.738 | loop fusion | bytes 24576 | tf_op jit(solution)/shard_map/slice | solution.py:25
  19.4 0.7 fusion.279
  20.1 2.3 %fusion.370 = f32[1,16,16,128]{3,2,1,0:T(8,128)S(1)} fusion(f32[1,16,16,128]{3,2,1,0:T(8,128)S(1)} %bitcast.93, f32[16,16,128]{2,1,0:T(8,128)S(1)} %fusion.279, f32[16,16]{1,0:T(8,128)S(1)} %get-tuple-element.6, f32[16,16]{1,0:T(8,128)S(1)} %get-tuple-element.7, f32[16,16]{1,0:T(8,128)S(1)} %get-tuple-element.8, f32[16,16]{1,0:T(8,128)S(1)} %get-tuple-element.9, ...), kind=kLoop, calls=%fused_computation.629 | loop fusion | flops 1998848 | bytes 424960 | tf_op jit(solution)/shard_map/add | solution.py:26
  22.4 1.5 %collective-permute-start.2 = (f32[1,15,16,128]{3,2,1,0:T(8,128)S(1)}, f32[1,15,16,128]{3,2,1,0:T(8,128)S(1)}, u32[]{:S(2)}, u32[]{:S(2)}) collective-permute-start(f32[1,15,16,128]{3,2,1,0:T(8,128)S(1)} %get-tuple-element.102), channel_id=1, source_target_pairs={{0,1},{1,2},{2,3},{4,5},{5,6},{6,7},{8,9},{9,10},{10,11},{12,13},{... | collective-permute-start | bytes 368648 | tf_op jit(solution)/shard_map/ppermute | solution.py:14
  23.9 1.4 %collective-permute-start.3 = (f32[1,15,16,128]{3,2,1,0:T(8,128)S(1)}, f32[1,15,16,128]{3,2,1,0:T(8,128)S(1)}, u32[]{:S(2)}, u32[]{:S(2)}) collective-permute-start(f32[1,15,16,128]{3,2,1,0:T(8,128)S(1)} %get-tuple-element.103), channel_id=1, source_target_pairs={{1,0},{2,1},{3,2},{5,4},{6,5},{7,6},{9,8},{10,9},{11,10},{13,12},{... | collective-permute-start | bytes 368648 | tf_op jit(solution)/shard_map/ppermute | solution.py:15
  25.4 3.8 %collective-permute-done.3 = f32[1,15,16,128]{3,2,1,0:T(8,128)S(1)} collective-permute-done((f32[1,15,16,128]{3,2,1,0:T(8,128)S(1)}, f32[1,15,16,128]{3,2,1,0:T(8,128)S(1)}, u32[]{:S(2)}, u32[]{:S(2)}) %collective-permute-start.3) | collective-permute-done | bytes 122912 | tf_op jit(solution)/shard_map/ppermute | solution.py:15
  29.3 0.3 fusion.90
  29.6 1.3 %collective-permute-start.4 = (f32[1,15,16,128]{3,2,1,0:T(8,128)S(1)}, f32[1,15,16,128]{3,2,1,0:T(8,128)S(1)}, u32[]{:S(2)}, u32[]{:S(2)}) collective-permute-start(f32[1,15,16,128]{3,2,1,0:T(8,128)S(1)} %get-tuple-element.100), channel_id=1, source_target_pairs={{1,0},{2,1},{3,2},{5,4},{6,5},{7,6},{9,8},{10,9},{11,10},{13,12},{... | collective-permute-start | bytes 368648 | tf_op jit(solution)/shard_map/ppermute | solution.py:15
  30.9 6.0 %collective-permute-start.5 = (f32[1,15,16,128]{3,2,1,0:T(8,128)S(1)}, f32[1,15,16,128]{3,2,1,0:T(8,128)S(1)}, u32[]{:S(2)}, u32[]{:S(2)}) collective-permute-start(f32[1,15,16,128]{3,2,1,0:T(8,128)S(1)} %get-tuple-element.101), channel_id=1, source_target_pairs={{0,1},{1,2},{2,3},{4,5},{5,6},{6,7},{8,9},{9,10},{10,11},{12,13},{... | collective-permute-start | bytes 368648 | tf_op jit(solution)/shard_map/ppermute | solution.py:14
  36.9 0.9 %collective-permute-done.5 = f32[1,15,16,128]{3,2,1,0:T(8,128)S(1)} collective-permute-done((f32[1,15,16,128]{3,2,1,0:T(8,128)S(1)}, f32[1,15,16,128]{3,2,1,0:T(8,128)S(1)}, u32[]{:S(2)}, u32[]{:S(2)}) %collective-permute-start.5) | collective-permute-done | bytes 122912 | tf_op jit(solution)/shard_map/ppermute | solution.py:14
  38.2 2.3 %fusion.430 = f32[1,16,16,128]{3,2,1,0:T(8,128)S(1)} fusion(f32[1,16,16,128]{3,2,1,0:T(8,128)S(1)} %fusion.3, f32[16,16]{1,0:T(8,128)S(1)} %get-tuple-element.21, f32[16,16]{1,0:T(8,128)S(1)} %get-tuple-element.6, f32[16,16]{1,0:T(8,128)S(1)} %get-tuple-element.7, f32[16,16]{1,0:T(8,128)S(1)} %get-tuple-element.8, f32[16,16]{1,0:T(8,128)S(1)} %get-tuple-element.9, ...), kind=kLoop, calls=%fused_computation.689 | loop fusion | flops 1998848 | bytes 293888 | tf_op jit(solution)/shard_map/add | solution.py:26
  40.5 1.3 %collective-permute-start.6 = (f32[1,16,15,128]{3,2,1,0:T(8,128)S(1)}, f32[1,16,15,128]{3,2,1,0:T(8,128)S(1)}, u32[]{:S(2)}, u32[]{:S(2)}) collective-permute-start(f32[1,16,15,128]{3,2,1,0:T(8,128)S(1)} %get-tuple-element.98), channel_id=1, source_target_pairs={{4,0},{8,4},{12,8},{5,1},{9,5},{13,9},{6,2},{10,6},{14,10},{7,3},{... | collective-permute-start | bytes 368648 | tf_op jit(solution)/shard_map/ppermute | solution.py:15
  41.8 4.6 %collective-permute-start.7 = (f32[1,16,15,128]{3,2,1,0:T(8,128)S(1)}, f32[1,16,15,128]{3,2,1,0:T(8,128)S(1)}, u32[]{:S(2)}, u32[]{:S(2)}) collective-permute-start(f32[1,16,15,128]{3,2,1,0:T(8,128)S(1)} %get-tuple-element.99), channel_id=1, source_target_pairs={{0,4},{4,8},{8,12},{1,5},{5,9},{9,13},{2,6},{6,10},{10,14},{3,7},{... | collective-permute-start | bytes 368648 | tf_op jit(solution)/shard_map/ppermute | solution.py:14
  46.4 1.0 %collective-permute-done.6 = f32[1,16,15,128]{3,2,1,0:T(8,128)S(1)} collective-permute-done((f32[1,16,15,128]{3,2,1,0:T(8,128)S(1)}, f32[1,16,15,128]{3,2,1,0:T(8,128)S(1)}, u32[]{:S(2)}, u32[]{:S(2)}) %collective-permute-start.6) | collective-permute-done | bytes 122912 | tf_op jit(solution)/shard_map/ppermute | solution.py:15
  47.4 1.5 %collective-permute-done.7 = f32[1,16,15,128]{3,2,1,0:T(8,128)S(1)} collective-permute-done((f32[1,16,15,128]{3,2,1,0:T(8,128)S(1)}, f32[1,16,15,128]{3,2,1,0:T(8,128)S(1)}, u32[]{:S(2)}, u32[]{:S(2)}) %collective-permute-start.7) | collective-permute-done | bytes 122912 | tf_op jit(solution)/shard_map/ppermute | solution.py:14
  48.9 1.4 %fusion.177 = f32[16,16,128]{2,1,0:T(8,128)} fusion(f32[1,16,15,128]{3,2,1,0:T(8,128)S(1)} %collective-permute-done.7, f32[1,16,16,128]{3,2,1,0:T(8,128)S(1)} %fusion.430, f32[1,16,15,128]{3,2,1,0:T(8,128)S(1)} %collective-permute-done.6, f32[16,128]{1,0:T(8,128)S(1)} %bitcast.97, f32[16,128]{1,0:T(8,128)S(1)} %bitcast.99, f32[16,128]{1,0:T(8,128)S(1)} %bitcast.101, ...), kind=kLoop, calls=%fused_computation.436 | loop fusion | flops 2981888 | bytes 761856 | tf_op jit(solution)/shard_map/reduce_sum | solution.py:62
  50.2 27.3 %all-reduce.4.cloned.1.call-done = f32[16,16,128]{2,1,0:T(8,128)} async-done(((f32[16,16,128]{2,1,0:T(8,128)}), f32[16,16,128]{2,1,0:T(8,128)}) %all-reduce.4.cloned.1.call-update) | async-done | bytes 131088 | tf_op jit(solution)/shard_map/psum | solution.py:63
  77.5 1.6 %multiply_multiply_fusion = f32[16,16,128]{2,1,0:T(8,128)} fusion(f32[16,16,128]{2,1,0:T(8,128)S(1)} %copy-done, f32[16,16,128]{2,1,0:T(8,128)} %all-reduce.4.cloned.1.call-done), kind=kLoop, calls=%fused_computation.757 | loop fusion | flops 65536 | bytes 393216 | tf_op jit(solution)/shard_map/div | solution.py:64
  (31 shorter events, 1.8 us)
Async XLA Ops:
  6.5 7.9 %copy-start.2 = (f32[1,3,16,31]{3,2,1,0:T(8,128)S(1)}, f32[1,3,16,31]{3,2,1,0:T(8,128)}, u32[]{:S(2)}) copy-start(f32[1,3,16,31]{3,2,1,0:T(8,128)} %param.11) | copy-start | bytes 17860
  6.5 71.0 %all-reduce.4.cloned.1.call-start = ((), (), s32[]{:S(2)}) async-start(), calls=%async_computation | async-start | bytes 262144 | tf_op jit(solution)/shard_map/psum | solution.py:63
  7.5 11.9 %collective-permute-start.1 = (f32[16,15,128]{2,1,0:T(8,128)S(1)}, f32[16,15,128]{2,1,0:T(8,128)S(1)}, u32[]{:S(2)}, u32[]{:S(2)}) collective-permute-start(f32[16,15,128]{2,1,0:T(8,128)S(1)} %get-tuple-element.104), channel_id=1, source_target_pairs={{4,0},{8,4},{12,8},{5,1},{9,5},{13,9},{6,2},{10,6},{14,10},{7,3},{... | collective-permute-start | bytes 368648 | tf_op jit(solution)/shard_map/ppermute | solution.py:15
  8.8 10.6 %collective-permute-start = (f32[16,15,128]{2,1,0:T(8,128)S(1)}, f32[16,15,128]{2,1,0:T(8,128)S(1)}, u32[]{:S(2)}, u32[]{:S(2)}) collective-permute-start(f32[16,15,128]{2,1,0:T(8,128)S(1)} %get-tuple-element.105), channel_id=1, source_target_pairs={{0,4},{4,8},{8,12},{1,5},{5,9},{9,13},{2,6},{6,10},{10,14},{3,7},{... | collective-permute-start | bytes 368648 | tf_op jit(solution)/shard_map/ppermute | solution.py:14
  14.5 0.7 copy-start.3
  15.7 0.7 copy-start.4
  16.6 1.4 %copy-start.5 = (s32[1,16,128]{2,1,0:T(8,128)S(1)}, s32[1,16,128]{2,1,0:T(8,128)}, u32[]{:S(2)}) copy-start(s32[1,16,128]{2,1,0:T(8,128)} %param.10) | copy-start | bytes 24580
  18.4 0.9 %copy-start = (f32[16,16,128]{2,1,0:T(8,128)S(1)}, f32[16,16,128]{2,1,0:T(8,128)}, u32[]{:S(2)}) copy-start(f32[16,16,128]{2,1,0:T(8,128)} %param.6) | copy-start | bytes 393220
  22.4 3.0 %collective-permute-start.2 = (f32[1,15,16,128]{3,2,1,0:T(8,128)S(1)}, f32[1,15,16,128]{3,2,1,0:T(8,128)S(1)}, u32[]{:S(2)}, u32[]{:S(2)}) collective-permute-start(f32[1,15,16,128]{3,2,1,0:T(8,128)S(1)} %get-tuple-element.102), channel_id=1, source_target_pairs={{0,1},{1,2},{2,3},{4,5},{5,6},{6,7},{8,9},{9,10},{10,11},{12,13},{... | collective-permute-start | bytes 368648 | tf_op jit(solution)/shard_map/ppermute | solution.py:14
  23.9 5.4 %copy-start.1 = (f32[1,16,16,128]{3,2,1,0:T(8,128)S(1)}, f32[1,16,16,128]{3,2,1,0:T(8,128)}, u32[]{:S(2)}) copy-start(f32[1,16,16,128]{3,2,1,0:T(8,128)} %param.7) | copy-start | bytes 393220
  23.9 5.4 %collective-permute-start.3 = (f32[1,15,16,128]{3,2,1,0:T(8,128)S(1)}, f32[1,15,16,128]{3,2,1,0:T(8,128)S(1)}, u32[]{:S(2)}, u32[]{:S(2)}) collective-permute-start(f32[1,15,16,128]{3,2,1,0:T(8,128)S(1)} %get-tuple-element.103), channel_id=1, source_target_pairs={{1,0},{2,1},{3,2},{5,4},{6,5},{7,6},{9,8},{10,9},{11,10},{13,12},{... | collective-permute-start | bytes 368648 | tf_op jit(solution)/shard_map/ppermute | solution.py:15
  29.6 7.3 %collective-permute-start.4 = (f32[1,15,16,128]{3,2,1,0:T(8,128)S(1)}, f32[1,15,16,128]{3,2,1,0:T(8,128)S(1)}, u32[]{:S(2)}, u32[]{:S(2)}) collective-permute-start(f32[1,15,16,128]{3,2,1,0:T(8,128)S(1)} %get-tuple-element.100), channel_id=1, source_target_pairs={{1,0},{2,1},{3,2},{5,4},{6,5},{7,6},{9,8},{10,9},{11,10},{13,12},{... | collective-permute-start | bytes 368648 | tf_op jit(solution)/shard_map/ppermute | solution.py:15
  30.9 7.0 %collective-permute-start.5 = (f32[1,15,16,128]{3,2,1,0:T(8,128)S(1)}, f32[1,15,16,128]{3,2,1,0:T(8,128)S(1)}, u32[]{:S(2)}, u32[]{:S(2)}) collective-permute-start(f32[1,15,16,128]{3,2,1,0:T(8,128)S(1)} %get-tuple-element.101), channel_id=1, source_target_pairs={{0,1},{1,2},{2,3},{4,5},{5,6},{6,7},{8,9},{9,10},{10,11},{12,13},{... | collective-permute-start | bytes 368648 | tf_op jit(solution)/shard_map/ppermute | solution.py:14
  40.5 6.9 %collective-permute-start.6 = (f32[1,16,15,128]{3,2,1,0:T(8,128)S(1)}, f32[1,16,15,128]{3,2,1,0:T(8,128)S(1)}, u32[]{:S(2)}, u32[]{:S(2)}) collective-permute-start(f32[1,16,15,128]{3,2,1,0:T(8,128)S(1)} %get-tuple-element.98), channel_id=1, source_target_pairs={{4,0},{8,4},{12,8},{5,1},{9,5},{13,9},{6,2},{10,6},{14,10},{7,3},{... | collective-permute-start | bytes 368648 | tf_op jit(solution)/shard_map/ppermute | solution.py:15
  41.8 7.1 %collective-permute-start.7 = (f32[1,16,15,128]{3,2,1,0:T(8,128)S(1)}, f32[1,16,15,128]{3,2,1,0:T(8,128)S(1)}, u32[]{:S(2)}, u32[]{:S(2)}) collective-permute-start(f32[1,16,15,128]{3,2,1,0:T(8,128)S(1)} %get-tuple-element.99), channel_id=1, source_target_pairs={{0,4},{4,8},{8,12},{1,5},{5,9},{9,13},{2,6},{6,10},{10,14},{3,7},{... | collective-permute-start | bytes 368648 | tf_op jit(solution)/shard_map/ppermute | solution.py:14
Sparse Core Ops, SparseCore 0:
  50.4 27.1 all-reduce.3
where the time goes:
time: 86.4 us; the launch traced here: 85.9 us
  waiting for transfers between devices  34.6 us (40%)
  starting transfers between devices  22.9 us (27%)
  between operations  13.7 us (16%)
  other arithmetic  8.97 us (10%)
  local copies, waits for them, and re-layouts  4.95 us (6%)
    psum x1, waiting for transfers between devices, shards(): total = lax.psum(local_sum, 'view')  27.3 us
    ppermute x4, starting transfers between devices, with_halo(): before = lax.ppermute(last, axis, up)  17.6 us
    add x4, other arithmetic, banded(): total = term if total is None else total + term  5.56 us
    ppermute x4, starting transfers between devices, with_halo(): after = lax.ppermute(initial, axis, down)  5.3 us
    ppermute x4, waiting for transfers between devices, with_halo(): after = lax.ppermute(initial, axis, down)  4.84 us
    slice x6, local copies, waits for them, and re-layouts, banded(): weights[..., k] * lax.slice_in_dim(padded, start, start + count, axis=dim)  2.63 us
    ppermute x4, waiting for transfers between devices, with_halo(): before = lax.ppermute(last, axis, up)  2.44 us
  transfers between devices with their start and end apart: 9, of which 5 were waited for; matrix products, arithmetic and copies ran while one was open for 4% of the time, Pallas kernels for 0%

commit v1 on v0

--- a/solution.py
+++ b/solution.py
@@ -60,7 +60,7 @@
     margin = with_halo(back_y, (("tile", 2),), 15)
     back_x = banded(margin, x_taps, 2, True)
     local_sum = jnp.sum(back_x, axis=0)
-    total = lax.psum(local_sum, "view")
+    total = jnp.sum(lax.all_gather(local_sum, "view"), axis=0)
     return estimate * total / (views_here * lax.axis_size("view"))
 
 

time: 86.4 us -> 52.6 us (0.61)
  the two profiles are of different devices: /device:TPU:0 before, /device:TPU:30 now
where the time goes in v1:
time: 52.6 us; the launch traced here: 52.2 us
  starting transfers between devices  20.3 us (39%)
  waiting for transfers between devices  12.8 us (24%)
  other arithmetic  7.42 us (14%)
  blocking collectives  5.63 us (11%)
  local copies, waits for them, and re-layouts  4.95 us (9%)
  matrix products  0.86 us (2%)
    ppermute x4, starting transfers between devices, with_halo(): after = lax.ppermute(initial, axis, down)  13.9 us
    ppermute x4, waiting for transfers between devices, with_halo(): before = lax.ppermute(last, axis, up)  9.12 us
    ppermute x4, starting transfers between devices, with_halo(): before = lax.ppermute(last, axis, up)  6.43 us
    add x5, other arithmetic, banded(): total = term if total is None else total + term  6.24 us
    all_gather x1, blocking collectives, shards(): total = jnp.sum(lax.all_gather(local_sum, 'view'), axis=0)  5.63 us
    ppermute x4, waiting for transfers between devices, with_halo(): after = lax.ppermute(initial, axis, down)  3.64 us
    slice x6, local copies, waits for them, and re-layouts, banded(): weights[..., k] * lax.slice_in_dim(padded, start, start + count, axis=dim)  2.63 us
    unnamed x13, local copies, waits for them, and re-layouts  1.26 us
  transfers between devices with their start and end apart: 8, of which 7 were waited for; matrix products, arithmetic and copies ran while one was open for 7% of the time, Pallas kernels for 0%

profile of v1, /device:TPU:30, one launch (start us, length us, event | category | flops | bytes accessed | tf_op | source)
XLA Modules:
  0.0 52.2 jit_solution(4788085036501646261)
XLA Ops:
  0.0 1.0 %fusion.454 = (f32[16,15,128]{2,1,0:T(8,128)S(1)}, f32[16,15,128]{2,1,0:T(8,128)S(1)}) fusion(f32[16,16,128]{2,1,0:T(8,128)} %param.6), kind=kLoop, calls=%fused_computation.776 | loop fusion | bytes 491520 | tf_op jit(solution)/shard_map/slice | solution.py:13
  1.0 2.4 %collective-permute-start.1 = (f32[16,15,128]{2,1,0:T(8,128)S(1)}, f32[16,15,128]{2,1,0:T(8,128)S(1)}, u32[]{:S(2)}, u32[]{:S(2)}) collective-permute-start(f32[16,15,128]{2,1,0:T(8,128)S(1)} %get-tuple-element.104), channel_id=1, source_target_pairs={{4,0},{8,4},{12,8},{5,1},{9,5},{13,9},{6,2},{10,6},{14,10},{7,3},{... | collective-permute-start | bytes 368648 | tf_op jit(solution)/shard_map/ppermute | solution.py:15
  3.4 1.3 %collective-permute-start = (f32[16,15,128]{2,1,0:T(8,128)S(1)}, f32[16,15,128]{2,1,0:T(8,128)S(1)}, u32[]{:S(2)}, u32[]{:S(2)}) collective-permute-start(f32[16,15,128]{2,1,0:T(8,128)S(1)} %get-tuple-element.105), channel_id=1, source_target_pairs={{0,4},{4,8},{8,12},{1,5},{5,9},{9,13},{2,6},{6,10},{10,14},{3,7},{... | collective-permute-start | bytes 368648 | tf_op jit(solution)/shard_map/ppermute | solution.py:14
  4.9 0.6 %copy-done.3 = s32[1,16,128]{2,1,0:T(8,128)S(1)} copy-done((s32[1,16,128]{2,1,0:T(8,128)S(1)}, s32[1,16,128]{2,1,0:T(8,128)}, u32[]{:S(2)}) %copy-start.3) | copy-done | bytes 8216
  6.0 0.6 %copy-done.4 = s32[1,16,16]{2,1,0:T(8,128)S(1)} copy-done((s32[1,16,16]{2,1,0:T(8,128)S(1)}, s32[1,16,16]{2,1,0:T(8,128)}, u32[]{:S(2)}) %copy-start.4) | copy-done | bytes 1048
  6.9 1.3 %slice_reduce_fusion.30 = (f32[16,16]{1,0:T(8,128)S(1)}, f32[16,16]{1,0:T(8,128)S(1)}, f32[16,16]{1,0:T(8,128)S(1)}, f32[16,16]{1,0:T(8,128)S(1)}, f32[16,16]{1,...) fusion(f32[1,16,16,1,31]{4,2,1,3,0:T(8,128)S(1)} %convolution_b, ...), kind=kLoop, calls=%fused_computation.755 | loop fusion | bytes 38912 | tf_op jit(solution)/shard_map/slice | solution.py:25
  8.7 0.9 %slice_reduce_fusion.29 = (f32[16,16]{1,0:T(8,128)S(1)}, f32[16,16]{1,0:T(8,128)S(1)}, f32[16,16]{1,0:T(8,128)S(1)}, f32[16,16]{1,0:T(8,128)S(1)}, f32[16,16]{1,...) fusion(f32[1,16,16,1,31]{4,2,1,3,0:T(8,128)S(1)} %convolution_b, ...), kind=kLoop, calls=%fused_computation.737 | loop fusion | bytes 24576 | tf_op jit(solution)/shard_map/slice | solution.py:25
  9.7 0.6 %collective-permute-done = f32[16,15,128]{2,1,0:T(8,128)S(1)} collective-permute-done((f32[16,15,128]{2,1,0:T(8,128)S(1)}, f32[16,15,128]{2,1,0:T(8,128)S(1)}, u32[]{:S(2)}, u32[]{:S(2)}) %collective-permute-start) | collective-permute-done | bytes 122912 | tf_op jit(solution)/shard_map/ppermute | solution.py:14
  10.2 0.6 %fusion.278 = f32[16,16,128]{2,1,0:T(8,128)S(1)} fusion(f32[16,15,128]{2,1,0:T(8,128)S(1)} %collective-permute-done, f32[16,16,128]{2,1,0:T(8,128)S(1)} %copy-done, f32[16,31,128]{2,1,0:T(8,128)S(1)} %constant_dynamic-update-slice_fusion, f32[16,128]{1,0:T(8,128)S(1)} %bitcast.94, f32[16,128]{1,0:T(8,128)S(1)} %bitcast.96, f32[16,128]{1,0:T(8,128)S(1)} %bitcast.98, ...), kind=kLoop, calls=%fused_computation.537 | loop fusion | flops 2490368 | bytes 2605056 | tf_op jit(solution)/shard_map/add | solution.py:26
  10.9 2.3 %fusion.369 = f32[1,16,16,128]{3,2,1,0:T(8,128)S(1)} fusion(f32[1,16,16,128]{3,2,1,0:T(8,128)S(1)} %bitcast.91, f32[16,16,128]{2,1,0:T(8,128)S(1)} %fusion.278, f32[16,16]{1,0:T(8,128)S(1)} %get-tuple-element.6, f32[16,16]{1,0:T(8,128)S(1)} %get-tuple-element.7, f32[16,16]{1,0:T(8,128)S(1)} %get-tuple-element.8, f32[16,16]{1,0:T(8,128)S(1)} %get-tuple-element.9, ...), kind=kLoop, calls=%fused_computation.628 | loop fusion | flops 1998848 | bytes 424960 | tf_op jit(solution)/shard_map/add | solution.py:26
  13.2 1.9 %collective-permute-start.2 = (f32[1,15,16,128]{3,2,1,0:T(8,128)S(1)}, f32[1,15,16,128]{3,2,1,0:T(8,128)S(1)}, u32[]{:S(2)}, u32[]{:S(2)}) collective-permute-start(f32[1,15,16,128]{3,2,1,0:T(8,128)S(1)} %get-tuple-element.102), channel_id=1, source_target_pairs={{0,1},{1,2},{2,3},{4,5},{5,6},{6,7},{8,9},{9,10},{10,11},{12,13},{... | collective-permute-start | bytes 368648 | tf_op jit(solution)/shard_map/ppermute | solution.py:14
  15.1 3.8 %collective-permute-start.3 = (f32[1,15,16,128]{3,2,1,0:T(8,128)S(1)}, f32[1,15,16,128]{3,2,1,0:T(8,128)S(1)}, u32[]{:S(2)}, u32[]{:S(2)}) collective-permute-start(f32[1,15,16,128]{3,2,1,0:T(8,128)S(1)} %get-tuple-element.103), channel_id=1, source_target_pairs={{1,0},{2,1},{3,2},{5,4},{6,5},{7,6},{9,8},{10,9},{11,10},{13,12},{... | collective-permute-start | bytes 368648 | tf_op jit(solution)/shard_map/ppermute | solution.py:15
  19.4 1.9 %collective-permute-done.3 = f32[1,15,16,128]{3,2,1,0:T(8,128)S(1)} collective-permute-done((f32[1,15,16,128]{3,2,1,0:T(8,128)S(1)}, f32[1,15,16,128]{3,2,1,0:T(8,128)S(1)}, u32[]{:S(2)}, u32[]{:S(2)}) %collective-permute-start.3) | collective-permute-done | bytes 122912 | tf_op jit(solution)/shard_map/ppermute | solution.py:15
  21.7 3.8 %collective-permute-start.4 = (f32[1,15,16,128]{3,2,1,0:T(8,128)S(1)}, f32[1,15,16,128]{3,2,1,0:T(8,128)S(1)}, u32[]{:S(2)}, u32[]{:S(2)}) collective-permute-start(f32[1,15,16,128]{3,2,1,0:T(8,128)S(1)} %get-tuple-element.100), channel_id=1, source_target_pairs={{1,0},{2,1},{3,2},{5,4},{6,5},{7,6},{9,8},{10,9},{11,10},{13,12},{... | collective-permute-start | bytes 368648 | tf_op jit(solution)/shard_map/ppermute | solution.py:15
  25.5 1.9 %collective-permute-start.5 = (f32[1,15,16,128]{3,2,1,0:T(8,128)S(1)}, f32[1,15,16,128]{3,2,1,0:T(8,128)S(1)}, u32[]{:S(2)}, u32[]{:S(2)}) collective-permute-start(f32[1,15,16,128]{3,2,1,0:T(8,128)S(1)} %get-tuple-element.101), channel_id=1, source_target_pairs={{0,1},{1,2},{2,3},{4,5},{5,6},{6,7},{8,9},{9,10},{10,11},{12,13},{... | collective-permute-start | bytes 368648 | tf_op jit(solution)/shard_map/ppermute | solution.py:14
  27.9 3.8 %collective-permute-done.5 = f32[1,15,16,128]{3,2,1,0:T(8,128)S(1)} collective-permute-done((f32[1,15,16,128]{3,2,1,0:T(8,128)S(1)}, f32[1,15,16,128]{3,2,1,0:T(8,128)S(1)}, u32[]{:S(2)}, u32[]{:S(2)}) %collective-permute-start.5) | collective-permute-done | bytes 122912 | tf_op jit(solution)/shard_map/ppermute | solution.py:14
  32.0 2.3 %fusion.429 = f32[1,16,16,128]{3,2,1,0:T(8,128)S(1)} fusion(f32[1,16,16,128]{3,2,1,0:T(8,128)S(1)} %fusion.3, f32[16,16]{1,0:T(8,128)S(1)} %get-tuple-element.21, f32[16,16]{1,0:T(8,128)S(1)} %get-tuple-element.6, f32[16,16]{1,0:T(8,128)S(1)} %get-tuple-element.7, f32[16,16]{1,0:T(8,128)S(1)} %get-tuple-element.8, f32[16,16]{1,0:T(8,128)S(1)} %get-tuple-element.9, ...), kind=kLoop, calls=%fused_computation.688 | loop fusion | flops 1998848 | bytes 293888 | tf_op jit(solution)/shard_map/add | solution.py:26
  34.3 4.0 %collective-permute-start.6 = (f32[1,16,15,128]{3,2,1,0:T(8,128)S(1)}, f32[1,16,15,128]{3,2,1,0:T(8,128)S(1)}, u32[]{:S(2)}, u32[]{:S(2)}) collective-permute-start(f32[1,16,15,128]{3,2,1,0:T(8,128)S(1)} %get-tuple-element.98), channel_id=1, source_target_pairs={{4,0},{8,4},{12,8},{5,1},{9,5},{13,9},{6,2},{10,6},{14,10},{7,3},{... | collective-permute-start | bytes 368648 | tf_op jit(solution)/shard_map/ppermute | solution.py:15
  38.3 1.3 %collective-permute-start.7 = (f32[1,16,15,128]{3,2,1,0:T(8,128)S(1)}, f32[1,16,15,128]{3,2,1,0:T(8,128)S(1)}, u32[]{:S(2)}, u32[]{:S(2)}) collective-permute-start(f32[1,16,15,128]{3,2,1,0:T(8,128)S(1)} %get-tuple-element.99), channel_id=1, source_target_pairs={{0,4},{4,8},{8,12},{1,5},{5,9},{9,13},{2,6},{6,10},{10,14},{3,7},{... | collective-permute-start | bytes 368648 | tf_op jit(solution)/shard_map/ppermute | solution.py:14
  39.6 1.2 %collective-permute-done.6 = f32[1,16,15,128]{3,2,1,0:T(8,128)S(1)} collective-permute-done((f32[1,16,15,128]{3,2,1,0:T(8,128)S(1)}, f32[1,16,15,128]{3,2,1,0:T(8,128)S(1)}, u32[]{:S(2)}, u32[]{:S(2)}) %collective-permute-start.6) | collective-permute-done | bytes 122912 | tf_op jit(solution)/shard_map/ppermute | solution.py:15
  40.8 4.4 %collective-permute-done.7 = f32[1,16,15,128]{3,2,1,0:T(8,128)S(1)} collective-permute-done((f32[1,16,15,128]{3,2,1,0:T(8,128)S(1)}, f32[1,16,15,128]{3,2,1,0:T(8,128)S(1)}, u32[]{:S(2)}, u32[]{:S(2)}) %collective-permute-start.7) | collective-permute-done | bytes 122912 | tf_op jit(solution)/shard_map/ppermute | solution.py:14
  45.2 0.7 %fusion.176 = f32[1,16,16,128]{3,2,1,0:T(8,128)S(1)} fusion(f32[1,16,15,128]{3,2,1,0:T(8,128)S(1)} %collective-permute-done.7, f32[1,16,16,128]{3,2,1,0:T(8,128)S(1)} %fusion.429, f32[1,16,15,128]{3,2,1,0:T(8,128)S(1)} %collective-permute-done.6, f32[16,128]{1,0:T(8,128)S(1)} %bitcast.95, f32[16,128]{1,0:T(8,128)S(1)} %bitcast.97, ...), kind=kLoop, calls=%fused_computation.435 | loop fusion | flops 2981888 | bytes 761856 | tf_op jit(solution)/shard_map/add | solution.py:26
  45.9 5.6 %all_gather.4 = f32[2,16,16,128]{3,2,1,0:T(8,128)S(1)} all-gather(f32[1,16,16,128]{3,2,1,0:T(8,128)S(1)} %fusion.176), channel_id=1, replica_groups=mesh['view'=2,'tile'=4,'slab'=4] {'view'}, dimensions={0}, use_global_device_ids=true | all-gather | bytes 393216 | tf_op jit(solution)/shard_map/all_gather | solution.py:63
  51.5 0.7 %multiply_multiply_fusion = f32[16,16,128]{2,1,0:T(8,128)} fusion(f32[16,16,128]{2,1,0:T(8,128)S(1)} %copy-done, f32[16,16,128]{2,1,0:T(8,128)S(1)} %reduce_sum.20), kind=kLoop, calls=%fused_computation.756 | loop fusion | flops 65536 | bytes 393216 | tf_op jit(solution)/shard_map/div | solution.py:64
  (30 shorter events, 3.1 us)
Async XLA Ops:
  0.0 4.7 %copy-start.2 = (f32[1,3,16,31]{3,2,1,0:T(8,128)S(1)}, f32[1,3,16,31]{3,2,1,0:T(8,128)}, u32[]{:S(2)}) copy-start(f32[1,3,16,31]{3,2,1,0:T(8,128)} %param.11) | copy-start | bytes 17860
  1.0 8.6 %collective-permute-start.1 = (f32[16,15,128]{2,1,0:T(8,128)S(1)}, f32[16,15,128]{2,1,0:T(8,128)S(1)}, u32[]{:S(2)}, u32[]{:S(2)}) collective-permute-start(f32[16,15,128]{2,1,0:T(8,128)S(1)} %get-tuple-element.104), channel_id=1, source_target_pairs={{4,0},{8,4},{12,8},{5,1},{9,5},{13,9},{6,2},{10,6},{14,10},{7,3},{... | collective-permute-start | bytes 368648 | tf_op jit(solution)/shard_map/ppermute | solution.py:15
  3.4 6.9 %collective-permute-start = (f32[16,15,128]{2,1,0:T(8,128)S(1)}, f32[16,15,128]{2,1,0:T(8,128)S(1)}, u32[]{:S(2)}, u32[]{:S(2)}) collective-permute-start(f32[16,15,128]{2,1,0:T(8,128)S(1)} %get-tuple-element.105), channel_id=1, source_target_pairs={{0,4},{4,8},{8,12},{1,5},{5,9},{9,13},{2,6},{6,10},{10,14},{3,7},{... | collective-permute-start | bytes 368648 | tf_op jit(solution)/shard_map/ppermute | solution.py:14
  4.8 0.7 %copy-start.3 = (s32[1,16,128]{2,1,0:T(8,128)S(1)}, s32[1,16,128]{2,1,0:T(8,128)}, u32[]{:S(2)}) copy-start(s32[1,16,128]{2,1,0:T(8,128)} %param.8) | copy-start | bytes 24580
  5.9 0.7 %copy-start.4 = (s32[1,16,16]{2,1,0:T(8,128)S(1)}, s32[1,16,16]{2,1,0:T(8,128)}, u32[]{:S(2)}) copy-start(s32[1,16,16]{2,1,0:T(8,128)} %param.9) | copy-start | bytes 3076
  6.9 1.4 %copy-start.5 = (s32[1,16,128]{2,1,0:T(8,128)S(1)}, s32[1,16,128]{2,1,0:T(8,128)}, u32[]{:S(2)}) copy-start(s32[1,16,128]{2,1,0:T(8,128)} %param.10) | copy-start | bytes 24580
  8.7 0.9 %copy-start = (f32[16,16,128]{2,1,0:T(8,128)S(1)}, f32[16,16,128]{2,1,0:T(8,128)}, u32[]{:S(2)}) copy-start(f32[16,16,128]{2,1,0:T(8,128)} %param.6) | copy-start | bytes 393220
  13.2 6.2 %collective-permute-start.2 = (f32[1,15,16,128]{3,2,1,0:T(8,128)S(1)}, f32[1,15,16,128]{3,2,1,0:T(8,128)S(1)}, u32[]{:S(2)}, u32[]{:S(2)}) collective-permute-start(f32[1,15,16,128]{3,2,1,0:T(8,128)S(1)} %get-tuple-element.102), channel_id=1, source_target_pairs={{0,1},{1,2},{2,3},{4,5},{5,6},{6,7},{8,9},{9,10},{10,11},{12,13},{... | collective-permute-start | bytes 368648 | tf_op jit(solution)/shard_map/ppermute | solution.py:14
  15.1 6.2 %copy-start.1 = (f32[1,16,16,128]{3,2,1,0:T(8,128)S(1)}, f32[1,16,16,128]{3,2,1,0:T(8,128)}, u32[]{:S(2)}) copy-start(f32[1,16,16,128]{3,2,1,0:T(8,128)} %param.7) | copy-start | bytes 393220
  15.1 6.2 %collective-permute-start.3 = (f32[1,15,16,128]{3,2,1,0:T(8,128)S(1)}, f32[1,15,16,128]{3,2,1,0:T(8,128)S(1)}, u32[]{:S(2)}, u32[]{:S(2)}) collective-permute-start(f32[1,15,16,128]{3,2,1,0:T(8,128)S(1)} %get-tuple-element.103), channel_id=1, source_target_pairs={{1,0},{2,1},{3,2},{5,4},{6,5},{7,6},{9,8},{10,9},{11,10},{13,12},{... | collective-permute-start | bytes 368648 | tf_op jit(solution)/shard_map/ppermute | solution.py:15
  21.7 6.2 %collective-permute-start.4 = (f32[1,15,16,128]{3,2,1,0:T(8,128)S(1)}, f32[1,15,16,128]{3,2,1,0:T(8,128)S(1)}, u32[]{:S(2)}, u32[]{:S(2)}) collective-permute-start(f32[1,15,16,128]{3,2,1,0:T(8,128)S(1)} %get-tuple-element.100), channel_id=1, source_target_pairs={{1,0},{2,1},{3,2},{5,4},{6,5},{7,6},{9,8},{10,9},{11,10},{13,12},{... | collective-permute-start | bytes 368648 | tf_op jit(solution)/shard_map/ppermute | solution.py:15
  25.5 6.2 %collective-permute-start.5 = (f32[1,15,16,128]{3,2,1,0:T(8,128)S(1)}, f32[1,15,16,128]{3,2,1,0:T(8,128)S(1)}, u32[]{:S(2)}, u32[]{:S(2)}) collective-permute-start(f32[1,15,16,128]{3,2,1,0:T(8,128)S(1)} %get-tuple-element.101), channel_id=1, source_target_pairs={{0,1},{1,2},{2,3},{4,5},{5,6},{6,7},{8,9},{9,10},{10,11},{12,13},{... | collective-permute-start | bytes 368648 | tf_op jit(solution)/shard_map/ppermute | solution.py:14
  34.3 6.5 %collective-permute-start.6 = (f32[1,16,15,128]{3,2,1,0:T(8,128)S(1)}, f32[1,16,15,128]{3,2,1,0:T(8,128)S(1)}, u32[]{:S(2)}, u32[]{:S(2)}) collective-permute-start(f32[1,16,15,128]{3,2,1,0:T(8,128)S(1)} %get-tuple-element.98), channel_id=1, source_target_pairs={{4,0},{8,4},{12,8},{5,1},{9,5},{13,9},{6,2},{10,6},{14,10},{7,3},{... | collective-permute-start | bytes 368648 | tf_op jit(solution)/shard_map/ppermute | solution.py:15
  38.3 6.9 %collective-permute-start.7 = (f32[1,16,15,128]{3,2,1,0:T(8,128)S(1)}, f32[1,16,15,128]{3,2,1,0:T(8,128)S(1)}, u32[]{:S(2)}, u32[]{:S(2)}) collective-permute-start(f32[1,16,15,128]{3,2,1,0:T(8,128)S(1)} %get-tuple-element.99), channel_id=1, source_target_pairs={{0,4},{4,8},{8,12},{1,5},{5,9},{9,13},{2,6},{6,10},{10,14},{3,7},{... | collective-permute-start | bytes 368648 | tf_op jit(solution)/shard_map/ppermute | solution.py:14
